TPU v7x, 32 devices: a whole 2x2x4 slice. The times are simulated.
32 devices in a mesh: psg: 8 (over z, x), mp: 4 (over y, core).
Axes of the slice: x: 2, y: 2, z: 4, core: 2. Of those that a mesh axis runs over, the one named last changes fastest.
Arguments:
- tokens: bfloat16 [8192, 4096], P('psg'), may hold values from -6 to 6
- lengths: int32 [32], P('psg'), may hold values from 32 to 256, as said below
- assignment: int32 [32], P('psg'), may hold values from 0 to 3, as said below
- retrieval: float32 [32], P('psg'), may hold values from -8 to 306
- enc_gain: float32 [4096], replicated, may hold values from 0.25 to 1.75
- enc_qkv: bfloat16 [3, 4096, 2048], P(None, 'psg', 'mp'), may hold values from -0.09375 to 0.09375
- position_bias: float32 [32, 32], P('mp'), may hold values from -6 to 306
- enc_output: bfloat16 [2048, 4096], P('mp', 'psg'), may hold values from -0.125 to 0.125
- final_gain: float32 [4096], replicated, may hold values from 0.25 to 1.75
- embedding: bfloat16 [32128, 4096], P('mp', 'psg'), may hold values from -18 to 18
- dec_tokens: int32 [4, 2], replicated, may hold values from 0 to 32127
- dec_gain: float32 [4096], P('psg'), may hold values from 0.25 to 1.75
- cross_query: bfloat16 [4096, 2048], P('psg', 'mp'), may hold values from -0.0234375 to 0.0234375
- cross_keyval: bfloat16 [2, 4096, 2048], P(None, 'psg', 'mp'), may hold values from -0.09375 to 0.09375
- cross_output: bfloat16 [2048, 4096], P('mp', 'psg'), may hold values from -0.25 to 0.25
Outputs:
- encoded: bfloat16 [8192, 4096], P('psg', 'mp')
- decoded: bfloat16 [4, 2, 4096], P(None, None, ('psg', 'mp'))
Inputs may be any that keep to these rules, and one draw needn't show every extreme that they name: Passage p holds real tokens in its first lengths[p] slots and padding after them; in every draw all passages of some index of psg have 256 real tokens. `assignment`: every claim has exactly 8 passages.
All inputs are finite; a program needn't handle non-finite values.
Results may differ from a plain program's by a relative error of at most 0.013.
The roundings to bfloat16 on the way count: a program that leaves them out, or rounds other values in their place, can miss the bound.
Values may be sent and summed in bfloat16 or wider, within the bound.
No kernel may reach another device: no remote copies, remote signals or barrier semaphores. Data moves between devices by JAX's collectives and lax.ppermute only.
A program may use at most 128 MiB of HBM per device.

v0:
```python
import math
import jax
import jax.numpy as jnp
import numpy as np
from jax import lax
from jax.sharding import PartitionSpec as P

D = 4096
HEAD_DIM = 64
BUCKETS = 32
MAXDIST = 128
SEQ = 256
CLAIMS = 4
POS = 2
EPSILON = 1e-06
MASKED = -1e30
HIGHEST = lax.Precision.HIGHEST


def merged(value, axis, combine):
    everything = jax.tree.map(lambda part: lax.all_gather(part, axis), value)
    first = jax.tree.map(lambda part: part[0], everything)

    def turn(k, so_far):
        return combine(so_far, jax.tree.map(lambda part: part[k], everything))

    return lax.fori_loop(1, lax.axis_size(axis), turn, first)


def bucket_onehot(length, buckets, max_distance):
    halfway = buckets // 2
    exact_max = halfway // 2
    relative_list = list(range(-(length - 1), length))
    beyond_list = [
        min(
            halfway - 1,
            exact_max
            + math.floor(
                math.log(max(abs(shift), 1) / exact_max)
                / math.log(max_distance / exact_max)
                * (halfway - exact_max)
            ),
        )
        for shift in relative_list
    ]
    relative = np.array(relative_list)
    beyond = np.array(beyond_list)
    distance = np.abs(relative)
    bucket_ids = np.where(relative > 0, halfway, 0) + np.where(
        distance < exact_max, distance, beyond
    )
    return (bucket_ids[None, :] == np.arange(buckets)[:, None]).astype(np.float32)


def toeplitz(vectors):
    heads_count, width_all = vectors.shape
    length = (width_all + 1) // 2
    padded = jnp.concatenate([vectors, jnp.zeros((heads_count, 1), vectors.dtype)], axis=1)
    rolled = jnp.roll(padded, -(length - 1), axis=1)
    repeated = jnp.tile(rolled, (1, length))[:, : length * (2 * length - 1)]
    return repeated.reshape(heads_count, length, 2 * length - 1)[:, :, :length]


def rms_norm(values, norm_gain):
    values = values.astype(jnp.float32)
    inverse = lax.rsqrt(jnp.mean(values * values, axis=-1, keepdims=True) + EPSILON)
    return values * inverse * norm_gain


def combine_partial(first, second):
    first_max, first_total, first_acc = first
    second_max, second_total, second_acc = second
    joint_max = jnp.maximum(first_max, second_max)
    first_scale = jnp.exp(first_max - joint_max)
    second_scale = jnp.exp(second_max - joint_max)
    joint_total = first_total * first_scale + second_total * second_scale
    joint_acc = first_acc * first_scale[..., None] + second_acc * second_scale[..., None]
    return (joint_max, joint_total, joint_acc)


def shards(
    tokens,
    lengths,
    assignment,
    retrieval,
    enc_gain,
    enc_qkv,
    position_bias,
    enc_output,
    final_gain,
    embedding,
    dec_tokens,
    dec_gain,
    cross_query,
    cross_keyval,
    cross_output,
):
    tok_rows = tokens.shape[0]
    model_width = tokens.shape[1]
    passages_here = lengths.shape[0]
    width_here = enc_qkv.shape[1]
    inner_here = enc_qkv.shape[2]
    heads_here = inner_here // HEAD_DIM
    query_rows = CLAIMS * POS
    positions = jnp.arange(SEQ)
    groups_count = lax.axis_size("mp")
    normed = rms_norm(tokens, enc_gain).astype(jnp.bfloat16)
    projected = jnp.einsum(
        "td,kdc->ktc",
        normed,
        lax.all_gather(enc_qkv, "psg", axis=1, tiled=True),
        preferred_element_type=jnp.float32,
    )
    shaped = projected.astype(jnp.bfloat16).reshape(3, passages_here, SEQ, heads_here, HEAD_DIM)
    bias_table = jnp.dot(
        position_bias, jnp.asarray(bucket_onehot(SEQ, BUCKETS, MAXDIST)), precision=HIGHEST
    )
    pair_bias = toeplitz(bias_table)
    scores = (
        jnp.einsum("pihd,pjhd->phij", shaped[0], shaped[1], preferred_element_type=jnp.float32)
        + pair_bias[None]
    )
    valid_keys = positions[None, :] < lengths[:, None]
    scores = jnp.where(valid_keys[:, None, None, :], scores, MASKED)
    weights = jnp.exp(scores - jnp.max(scores, axis=-1, keepdims=True))
    probabilities = (weights / jnp.sum(weights, axis=-1, keepdims=True)).astype(jnp.bfloat16)
    attended = jnp.einsum(
        "phij,pjhd->pihd", probabilities, shaped[2], preferred_element_type=jnp.float32
    )
    attended = attended.astype(jnp.bfloat16).reshape(tok_rows, inner_here)
    share_width = model_width // groups_count
    share_start = lax.axis_index("mp") * share_width
    partial_out = jnp.dot(
        attended,
        lax.all_gather(enc_output, "psg", axis=1, tiled=True),
        preferred_element_type=jnp.float32,
    ).astype(jnp.bfloat16)
    summed = lax.psum(partial_out, "mp").astype(jnp.float32)
    encoded_full = (tokens.astype(jnp.float32) + summed).astype(jnp.bfloat16)
    encoded = lax.dynamic_slice_in_dim(encoded_full, share_start, share_width, 1)
    memory = rms_norm(encoded_full, final_gain).astype(jnp.bfloat16)
    vocab_here = embedding.shape[0]
    token_ids = dec_tokens.reshape(-1) - lax.axis_index("mp") * vocab_here
    lookup = (token_ids[:, None] == jnp.arange(vocab_here)[None, :]).astype(jnp.bfloat16)
    found_rows = jnp.dot(lookup, embedding, preferred_element_type=jnp.float32).astype(jnp.bfloat16)
    embedded = lax.psum(found_rows, "mp").astype(jnp.float32)
    query_weight = cross_query.astype(jnp.float32)
    squares_dec = lax.psum(jnp.sum(embedded * embedded, axis=1), "psg")
    dquery = embedded * lax.rsqrt(squares_dec / D + EPSILON)[:, None] * dec_gain
    cquery = lax.psum(jnp.dot(dquery, query_weight, precision=HIGHEST), "psg")
    cquery = cquery.reshape(query_rows, heads_here, HEAD_DIM)
    row_claim = jnp.arange(query_rows) // POS
    usable = (row_claim[:, None, None] == assignment[None, :, None]) & (
        positions[None, None, :] < lengths[None, :, None]
    )
    usable = usable.reshape(query_rows, 1, tok_rows)
    key_bias = jnp.broadcast_to(retrieval[:, None], (passages_here, SEQ)).reshape(tok_rows)
    key_weight = cross_keyval[0].astype(jnp.float32).reshape(width_here, heads_here, HEAD_DIM)
    folded = jnp.einsum("rhj,dhj->rhd", cquery, key_weight, precision=HIGHEST)
    folded_all = lax.all_gather(folded.astype(jnp.bfloat16), "psg", axis=2, tiled=True).astype(
        folded.dtype
    )
    memory_wide = memory.astype(jnp.float32)
    cross_scores = jnp.einsum("td,rhd->rht", memory_wide, folded_all, precision=HIGHEST) + key_bias
    masked = jnp.where(usable, cross_scores, MASKED)
    local_max = jnp.max(masked, axis=-1)
    weights_c = jnp.where(usable, jnp.exp(masked - local_max[..., None]), 0.0)
    local_max, weights_c = (local_max, weights_c)
    local_total = jnp.sum(weights_c, axis=-1)
    pooled = jnp.einsum("rht,td->rhd", weights_c, memory_wide, precision=HIGHEST)
    joint_max, joint_total, joint_pool = merged(
        (local_max, local_total, pooled), "psg", combine_partial
    )
    own_pool = (
        lax.dynamic_slice_in_dim(joint_pool, lax.axis_index("psg") * width_here, width_here, 2)
        / joint_total[..., None]
    )
    value_weight = cross_keyval[1].astype(jnp.float32).reshape(width_here, heads_here, HEAD_DIM)
    value_terms = jnp.einsum("rhd,dhj->rhj", own_pool, value_weight, precision=HIGHEST)
    cross_attn = lax.psum(value_terms, "psg")
    out_part = jnp.dot(
        cross_attn.reshape(query_rows, inner_here),
        cross_output.astype(jnp.float32),
        precision=HIGHEST,
    )
    out_share = lax.psum_scatter(out_part, "mp", scatter_dimension=1, tiled=True)
    piece_width = out_share.shape[1]
    residual = lax.dynamic_slice_in_dim(
        embedded, lax.axis_index("mp") * piece_width, piece_width, 1
    )
    decoded = (residual + out_share).astype(jnp.bfloat16).reshape(CLAIMS, POS, piece_width)
    return (encoded, decoded)


def solution(mesh):
    in_specs = (
        P("psg", None),
        P("psg"),
        P("psg"),
        P("psg"),
        P(),
        P(None, "psg", "mp"),
        P("mp", None),
        P("mp", "psg"),
        P(),
        P("mp", "psg"),
        P(),
        P("psg"),
        P("psg", "mp"),
        P(None, "psg", "mp"),
        P("mp", "psg"),
    )
    out_specs = (P("psg", "mp"), P(None, None, ("psg", "mp")))
    return jax.shard_map(shards, mesh=mesh, in_specs=in_specs, out_specs=out_specs, check_vma=False)
```

profile of v0, /device:TPU:0, one launch (start us, length us, event | category | flops | bytes accessed | tf_op | source)
XLA Modules:
  0.0 641.4 jit_solution(5036497669544402802)
XLA Ops:
  7.2 0.7 all-gather.7.cloned.1.call-update
  8.0 0.7 all-gather.9.cloned.1.call-update
  8.7 1.0 convolution_bitcast_fusion.1
  9.7 0.1 pad_slice_fusion
  9.8 0.1 pad_maximum_fusion
  9.9 0.5 tile.4
  10.4 2.2 slice.61
  12.6 7.9 %reshape.172 = f32[8,256,511]{2,1,0:T(8,128)} reshape(f32[8,130816]{1,0:T(8,128)} %slice.61) | data formatting | bytes 8372224 | tf_op jit(solution)/shard_map/reshape | solution.py:61
  20.5 2.2 slice.62
  22.7 2.1 copy.44
  24.9 5.1 fusion.7
  29.9 159.1 %all-gather.7.cloned.1.call-done = bf16[3,4096,512]{2,1,0:T(8,128)(2,1)} async-done(((bf16[3,512,512]{2,1,0:T(8,128)(2,1)}), bf16[3,4096,512]{2,1,0:T(8,128)(2,1)}) %all-gather.7.cloned.1.call-update) | async-done | bytes 12582928 | tf_op jit(solution)/shard_map/all_gather | solution.py:111
  189.0 18.3 %convert_bitcast_fusion = bf16[3,1024,512]{2,1,0:T(8,128)(2,1)S(1)} fusion(bf16[3,4096,512]{2,1,0:T(8,128)(2,1)} %all-gather.7.cloned.1.call-done, bf16[1024,4096]{1,0:T(8,128)(2,1)} %param.18, f32[4096]{0:T(1024)S(1)} %copy-done.10, f32[1024]{0:T(1024)S(1)} %add_rsqrt_fusion.1), kind=kOutput, calls=%fused_computation.37 | convolution fusion | flops 12903251968 | bytes 24137728 | tf_op jit(solution)/shard_map/td,kdc->ktc/dot_general | solution.py:108
  207.3 1.7 fusion.62
  209.1 2.8 reshape.191
  211.9 3.9 reshape.192
  215.8 3.9 reshape.190
  219.6 3.0 fusion.28
  222.7 5.4 fusion.64
  228.0 4.5 fusion.35
  232.5 0.8 copy.47
  233.3 0.2 copy.63
  233.5 30.4 %all-gather.9.cloned.1.call-done = bf16[512,4096]{1,0:T(8,128)(2,1)} async-done(((bf16[512,512]{1,0:T(8,128)(2,1)}), bf16[512,4096]{1,0:T(8,128)(2,1)}) %all-gather.9.cloned.1.call-update) | async-done | bytes 4194320 | tf_op jit(solution)/shard_map/all_gather | solution.py:135
  263.9 8.9 %convolution_convert_fusion = bf16[1024,4096]{1,0:T(8,128)(2,1)} fusion(bf16[1024,512]{0,1:T(8,128)(2,1)S(1)} %bitcast.81, bf16[512,4096]{1,0:T(8,128)(2,1)} %all-gather.9.cloned.1.call-done), kind=kOutput, calls=%fused_computation.29 | convolution fusion | flops 4299161600 | bytes 13631488 | tf_op jit(solution)/shard_map/dot_general | solution.py:133
  273.0 0.6 copy-done.7
  273.5 0.1 copy.48
  273.6 0.1 sub.57
  273.7 5.1 convolution_convert_fusion.2
  278.8 6.7 %psum.36 = bf16[8,512]{1,0:T(8,128)(2,1)S(1)} all-reduce(bf16[8,512]{1,0:T(8,128)(2,1)S(1)} %convolution_convert_fusion.2), channel_id=1, replica_groups=mesh['psg'=8,'mp'=4] {'mp'}, use_global_device_ids=true, to_apply=%region_4.5 | all-reduce | flops 4096 | bytes 16384 | tf_op jit(solution)/shard_map/psum | solution.py:146
  285.5 0.1 multiply_reduce_fusion
  285.7 19.2 %psum.37 = f32[8]{0:T(128)S(1)} all-reduce(f32[8]{0:T(128)S(1)} %multiply_reduce_fusion), channel_id=1, replica_groups=mesh['psg'=8,'mp'=4] {'psg'}, use_global_device_ids=true, to_apply=%region_6.7 | all-reduce | flops 8 | bytes 64 | tf_op jit(solution)/shard_map/psum | solution.py:148
  304.8 0.4 fusion.52
  305.2 0.1 reshape.174
  305.4 0.2 copy.62
  305.8 33.1 %psum.38 = f32[8,8,64]{2,0,1:T(8,128)S(1)} all-reduce(f32[8,8,64]{2,0,1:T(8,128)S(1)} %copy.49), channel_id=1, replica_groups=mesh['psg'=8,'mp'=4] {'psg'}, use_global_device_ids=true, to_apply=%region_7.8 | all-reduce | flops 4096 | bytes 32768 | tf_op jit(solution)/shard_map/psum | solution.py:150
  339.0 0.1 and.35
  339.1 0.3 fusion.44
  339.4 31.5 %all_gather.29 = bf16[8,8,4096]{2,0,1:T(8,128)(2,1)S(1)} all-gather(bf16[8,8,512]{2,0,1:T(8,128)(2,1)S(1)} %fusion.44), channel_id=1, replica_groups=mesh['psg'=8,'mp'=4] {'psg'}, dimensions={2}, use_global_device_ids=true | all-gather | bytes 589824 | tf_op jit(solution)/shard_map/all_gather | solution.py:160
  370.9 53.5 %all-reduce.3.cloned.1.call-done = bf16[1024,4096]{1,0:T(8,128)(2,1)} async-done(((bf16[1024,4096]{1,0:T(8,128)(2,1)}), bf16[1024,4096]{1,0:T(8,128)(2,1)}) %all-reduce.3.cloned.1.call-update) | async-done | bytes 8388624 | tf_op jit(solution)/shard_map/psum | solution.py:138
  424.4 7.8 %fusion.4 = (f32[1024]{0:T(1024)S(1)}, bf16[1024,4096]{1,0:T(8,128)(2,1)S(1)}) fusion(bf16[1024,4096]{1,0:T(8,128)(2,1)} %all-reduce.3.cloned.1.call-done, bf16[1024,4096]{1,0:T(8,128)(2,1)} %param.18), kind=kLoop, calls=%fused_computation.14 | loop fusion | flops 29359104 | bytes 25169920 | tf_op jit(solution)/shard_map/reduce_sum | solution.py:66
  432.2 2.9 fusion.65
  435.1 0.3 copy-done.1
  435.4 6.4 %fusion.18 = f32[8,8,4096]{2,1,0:T(8,128)} fusion(bf16[1024,4096]{1,0:T(8,128)(2,1)S(1)} %get-tuple-element.200, f32[4096]{0:T(1024)S(1)} %copy-done.11, f32[1024]{0:T(1024)S(1)} %add_rsqrt_fusion, f32[8,8,1024]{2,1,0:T(8,128)S(1)} %get-tuple-element.209, f32[8,8]{1,0:T(8,128)S(1)} %get-tuple-element.208, pred[8,1024]{1,0:T(8,128)(4,1)S(1)} %broadcast_and_fusion), kind=kOutput, calls=%fused_computation.31 | convolution fusion | flops 3238133760 | bytes 9728256 | tf_op jit(solution)/shard_map/rht,td->rhd/dot_general | solution.py:170
  441.9 0.2 copy.52
  442.1 0.2 fusion.46
  442.3 31.6 %all-gather.1 = f32[64,8]{1,0:T(8,128)S(1)} all-gather(f32[8,8]{1,0:T(8,128)S(1)} %fusion.46), channel_id=3, replica_groups=mesh['psg'=8,'mp'=4] {'psg'}, dimensions={0}, use_global_device_ids=true | all-gather | bytes 2304 | tf_op jit(solution)/shard_map/all_gather | solution.py:21
  474.0 31.6 %all-gather = f32[64,8]{1,0:T(8,128)S(1)} all-gather(f32[8,8]{1,0:T(8,128)S(1)} %get-tuple-element.208), channel_id=2, replica_groups=mesh['psg'=8,'mp'=4] {'psg'}, dimensions={0}, use_global_device_ids=true | all-gather | bytes 2304 | tf_op jit(solution)/shard_map/all_gather | solution.py:21
  505.6 61.5 %all-gather.11.cloned.1.call-done = f32[64,8,4096]{2,1,0:T(8,128)} async-done(((f32[8,8,4096]{2,1,0:T(8,128)}), f32[64,8,4096]{2,1,0:T(8,128)}) %all-gather.11.cloned.1.call-update) | async-done | bytes 8388624 | tf_op jit(solution)/shard_map/all_gather | solution.py:21
  567.1 1.3 slice.65
  568.4 12.4 %while.19 = (s32[]{:T(128)}, f32[8,8]{1,0:T(8,128)S(1)}, f32[8,8]{1,0:T(8,128)S(1)}, f32[8,8,4096]{2,1,0:T(8,128)S(1)}, f32[8,8,8]{2,1,0:T(8,128)S(1)}, /*index=...) while((s32[]{:T(128)}, f32[8,8]{1,0:T(8,128)S(1)}, ...), condition=%wide.region_12.13_spmd, body=%wide.region_11.12_spmd.sunk | while | flops 786821 | bytes 3148439 | solution.py:27
  568.4 1.8 fusion.82
  570.2 1.7 fusion.82
  572.0 1.7 fusion.82
  573.8 1.7 fusion.82
  575.5 1.7 fusion.82
  577.3 1.7 fusion.82
  579.1 1.7 fusion.82
  580.8 0.1 dynamic-slice_divide_fusion
  580.9 0.5 convolution_bitcast_fusion
  581.5 34.2 %psum.39 = f32[8,512]{1,0:T(8,128)S(1)} all-reduce(f32[8,512]{1,0:T(8,128)S(1)} %reshape.177), channel_id=1, replica_groups=mesh['psg'=8,'mp'=4] {'psg'}, use_global_device_ids=true, to_apply=%region_13.14 | all-reduce | flops 4096 | bytes 32768 | tf_op jit(solution)/shard_map/psum | solution.py:180
  615.8 0.9 fusion.66
  616.7 3.1 constant_dynamic-slice_fusion
  619.8 13.8 %reduce-scatter.2.cloned.1.call-done = f32[8,128]{1,0:T(8,128)} async-done(((f32[8,512]{1,0:T(8,128)}), f32[8,128]{1,0:T(8,128)}) %reduce-scatter.2.cloned.1.call-update) | async-done | bytes 4112 | tf_op jit(solution)/shard_map/reduce_scatter | solution.py:186
  633.6 1.3 add_convert_fusion
  (61 shorter events, 1.0 us)
Async XLA Ops:
  7.2 297.7 %copy-start = (bf16[512,512]{1,0:T(8,128)(2,1)S(1)}, bf16[512,512]{1,0:T(8,128)(2,1)}, u32[]{:S(2)}) copy-start(bf16[512,512]{1,0:T(8,128)(2,1)} %param.30) | copy-start | bytes 1572868
  7.2 181.8 %all-gather.7.cloned.1.call-start = ((), (), s32[]{:S(2)}) async-start(), calls=%async_computation.1 | async-start | bytes 14155776 | tf_op jit(solution)/shard_map/all_gather | solution.py:111
  7.9 256.0 %all-gather.9.cloned.1.call-start = ((), (), s32[]{:S(2)}) async-start(), calls=%async_computation.2 | async-start | bytes 4718592 | tf_op jit(solution)/shard_map/all_gather | solution.py:135
  8.7 415.7 %all-reduce.3.cloned.1.call-start = ((), (), s32[]{:S(2)}) async-start(), calls=%async_computation.3 | async-start | bytes 16777216 | tf_op jit(solution)/shard_map/psum | solution.py:138
  12.6 12.1 %copy-start.9 = (s32[4]{0:T(128)S(1)}, s32[4]{0:T(128)}, u32[]{:S(2)}) copy-start(s32[4]{0:T(128)} %param.19) | copy-start | bytes 52
  20.5 168.5 %copy-start.10 = (f32[4096]{0:T(1024)S(1)}, f32[4096]{0:T(1024)}, u32[]{:S(2)}) copy-start(f32[4096]{0:T(1024)} %param.22) | copy-start | bytes 49156
  219.6 3.0 copy-start.3
  222.7 5.4 copy-start.2
  272.8 0.7 copy-start.7
  272.9 32.0 %copy-start.6 = (f32[512]{0:T(512)S(1)}, f32[512]{0:T(512)}, u32[]{:S(2)}) copy-start(f32[512]{0:T(512)} %param.29) | copy-start | bytes 6148
  272.9 32.4 %copy-start.4 = (bf16[2,512,512]{2,1,0:T(8,128)(2,1)S(1)}, bf16[2,512,512]{2,1,0:T(8,128)(2,1)}, u32[]{:S(2)}) copy-start(bf16[2,512,512]{2,1,0:T(8,128)(2,1)} %param.31) | copy-start | bytes 3145732
  272.9 294.2 %all-gather.11.cloned.1.call-start = ((), (), s32[]{:S(2)}) async-start(), calls=%async_computation.5 | async-start | bytes 9437184 | tf_op jit(solution)/shard_map/all_gather | solution.py:21
  273.7 31.9 %copy-start.8 = (f32[4]{0:T(128)S(1)}, f32[4]{0:T(128)}, u32[]{:S(2)}) copy-start(f32[4]{0:T(128)} %param.21) | copy-start | bytes 52
  273.7 65.2 %copy-start.12 = (s32[4]{0:T(128)S(1)}, s32[4]{0:T(128)}, u32[]{:S(2)}) copy-start(s32[4]{0:T(128)} %param.20) | copy-start | bytes 52
  370.9 61.3 %copy-start.11 = (f32[4096]{0:T(1024)S(1)}, f32[4096]{0:T(1024)}, u32[]{:S(2)}) copy-start(f32[4096]{0:T(1024)} %param.26) | copy-start | bytes 49156
  432.2 3.2 copy-start.1
  441.9 191.8 %reduce-scatter.2.cloned.1.call-start = ((), (), s32[]{:S(2)}) async-start(), calls=%async_computation.4 | async-start | bytes 20480 | tf_op jit(solution)/shard_map/reduce_scatter | solution.py:186
  568.4 47.4 %copy-start.5 = (bf16[512,512]{1,0:T(8,128)(2,1)S(1)}, bf16[512,512]{1,0:T(8,128)(2,1)}, u32[]{:S(2)}) copy-start(bf16[512,512]{1,0:T(8,128)(2,1)} %param.32) | copy-start | bytes 1572868
Sparse Core Ops, SparseCore 0:
  10.2 178.8 all-gather.6
  191.1 72.8 all-gather.8
  273.0 151.3 all-reduce.2
  442.0 125.0 all-gather.10
  616.8 16.7 reduce-scatter.1
where the time goes:
time: 642 us; the launch traced here: 641 us
  waiting for transfers between devices  320 us (50%)
  blocking collectives  188 us (29%)
  matrix products  52.2 us (8%)
  local copies, waits for them, and re-layouts  34.7 us (5%)
  other arithmetic  32.4 us (5%)
  between operations  14.1 us (2%)
    all_gather x1, waiting for transfers between devices, shards(): lax.all_gather(enc_qkv, 'psg', axis=1, tiled=True)  159 us
    all_gather x2, blocking collectives, merged(): everything = jax.tree.map(lambda part: lax.all_gather(part, axis), value)  63.2 us
    all_gather x1, waiting for transfers between devices, merged(): everything = jax.tree.map(lambda part: lax.all_gather(part, axis), value)  61.5 us
    psum x1, waiting for transfers between devices, shards(): summed = lax.psum(partial_out, 'mp').astype(jnp.float32)  53.5 us
    psum x1, blocking collectives, shards(): cross_attn = lax.psum(value_terms, 'psg')  34.2 us
    psum x1, blocking collectives, shards(): cquery = lax.psum(jnp.dot(dquery, query_weight, precision=HIGHEST), 'psg')  33.1 us
    all_gather x1, blocking collectives, shards(): lax.all_gather(folded.astype(jnp.bfloat16), 'psg', axis=2, tiled=True)  31.5 us
    all_gather x1, waiting for transfers between devices, shards(): lax.all_gather(enc_output, 'psg', axis=1, tiled=True)  30.4 us
  transfers between devices with their start and end apart: 5, of which 5 were waited for; matrix products, arithmetic and copies ran while one was open for 12% of the time, Pallas kernels for 0%

commit v1 on v0

--- a/solution.py
+++ b/solution.py
@@ -15,6 +15,14 @@
 EPSILON = 1e-06
 MASKED = -1e30
 HIGHEST = lax.Precision.HIGHEST
+
+
+def doubling_sum(x, name):
+    size, total = (lax.axis_size(name), x)
+    for stride in [1 << k for k in range(size.bit_length() - 1)]:
+        swap = [(i, i ^ stride) for i in range(size)]
+        total = total + lax.ppermute(total, name, swap)
+    return total
 
 
 def merged(value, axis, combine):
@@ -177,7 +185,7 @@
     )
     value_weight = cross_keyval[1].astype(jnp.float32).reshape(width_here, heads_here, HEAD_DIM)
     value_terms = jnp.einsum("rhd,dhj->rhj", own_pool, value_weight, precision=HIGHEST)
-    cross_attn = lax.psum(value_terms, "psg")
+    cross_attn = doubling_sum(value_terms, "psg")
     out_part = jnp.dot(
         cross_attn.reshape(query_rows, inner_here),
         cross_output.astype(jnp.float32),

time: 642 us -> 622 us (0.969)
  blocking collectives: 188 us -> 154 us
  waiting for transfers between devices: 320 us -> 331 us
    psum x1 -> x0, blocking collectives: 34.2 us -> none  [shards(): cross_attn = lax.psum(value_terms, 'psg')]
    ppermute x0 -> x3, waiting for transfers between devices: none -> 10.6 us  [doubling_sum(): total = total + lax.ppermute(total, name, swap)]
  transfers between devices with their start and end apart: 5 -> 8, of which waited for: 5 -> 8; matrix products, arithmetic and copies ran while one was open for 12% -> 12% of each run, Pallas kernels for 0% -> 0%
where the time goes in v1:
time: 622 us; the launch traced here: 621 us
  waiting for transfers between devices  331 us (53%)
  blocking collectives  154 us (25%)
  matrix products  52.3 us (8%)
  local copies, waits for them, and re-layouts  34.6 us (6%)
  other arithmetic  32.4 us (5%)
  between operations  14 us (2%)
    all_gather x1, waiting for transfers between devices, shards(): lax.all_gather(enc_qkv, 'psg', axis=1, tiled=True)  159 us
    all_gather x2, blocking collectives, merged(): everything = jax.tree.map(lambda part: lax.all_gather(part, axis), value)  63.1 us
    all_gather x1, waiting for transfers between devices, merged(): everything = jax.tree.map(lambda part: lax.all_gather(part, axis), value)  61.6 us
    psum x1, waiting for transfers between devices, shards(): summed = lax.psum(partial_out, 'mp').astype(jnp.float32)  53.5 us
    psum x1, blocking collectives, shards(): cquery = lax.psum(jnp.dot(dquery, query_weight, precision=HIGHEST), 'psg')  33.1 us
    all_gather x1, blocking collectives, shards(): lax.all_gather(folded.astype(jnp.bfloat16), 'psg', axis=2, tiled=True)  31.5 us
    all_gather x1, waiting for transfers between devices, shards(): lax.all_gather(enc_output, 'psg', axis=1, tiled=True)  30.4 us
    psum x1, blocking collectives, shards(): squares_dec = lax.psum(jnp.sum(embedded * embedded, axis=1), 'psg')  19.2 us
  transfers between devices with their start and end apart: 8, of which 8 were waited for; matrix products, arithmetic and copies ran while one was open for 12% of the time, Pallas kernels for 0%

profile of v1, /device:TPU:0, one launch (start us, length us, event | category | flops | bytes accessed | tf_op | source)
XLA Modules:
  0.0 620.8 jit_solution(15320351865871725227)
XLA Ops:
  7.2 0.7 all-gather.7.cloned.1.call-update
  8.0 0.7 all-gather.9.cloned.1.call-update
  8.7 1.0 convolution_bitcast_fusion.1
  9.9 0.5 tile.4
  10.4 2.2 slice.61
  12.7 7.9 %reshape.172 = f32[8,256,511]{2,1,0:T(8,128)} reshape(f32[8,130816]{1,0:T(8,128)} %slice.61) | data formatting | bytes 8372224 | tf_op jit(solution)/shard_map/reshape | solution.py:69
  20.5 2.2 slice.62
  22.7 2.0 copy.44
  24.9 5.1 fusion.7
  29.9 159.1 %all-gather.7.cloned.1.call-done = bf16[3,4096,512]{2,1,0:T(8,128)(2,1)} async-done(((bf16[3,512,512]{2,1,0:T(8,128)(2,1)}), bf16[3,4096,512]{2,1,0:T(8,128)(2,1)}) %all-gather.7.cloned.1.call-update) | async-done | bytes 12582928 | tf_op jit(solution)/shard_map/all_gather | solution.py:119
  189.0 18.3 %convert_bitcast_fusion = bf16[3,1024,512]{2,1,0:T(8,128)(2,1)S(1)} fusion(bf16[3,4096,512]{2,1,0:T(8,128)(2,1)} %all-gather.7.cloned.1.call-done, bf16[1024,4096]{1,0:T(8,128)(2,1)} %param.18, f32[4096]{0:T(1024)S(1)} %copy-done.10, f32[1024]{0:T(1024)S(1)} %add_rsqrt_fusion.1), kind=kOutput, calls=%fused_computation.37 | convolution fusion | flops 12903251968 | bytes 24137728 | tf_op jit(solution)/shard_map/td,kdc->ktc/dot_general | solution.py:116
  207.3 1.7 fusion.62
  209.1 2.8 reshape.191
  211.9 3.9 reshape.192
  215.7 3.9 reshape.190
  219.6 3.0 fusion.28
  222.6 5.4 fusion.64
  228.0 4.5 fusion.35
  232.5 0.8 copy.47
  233.3 0.2 copy.63
  233.5 30.4 %all-gather.9.cloned.1.call-done = bf16[512,4096]{1,0:T(8,128)(2,1)} async-done(((bf16[512,512]{1,0:T(8,128)(2,1)}), bf16[512,4096]{1,0:T(8,128)(2,1)}) %all-gather.9.cloned.1.call-update) | async-done | bytes 4194320 | tf_op jit(solution)/shard_map/all_gather | solution.py:143
  263.9 8.9 %convolution_convert_fusion = bf16[1024,4096]{1,0:T(8,128)(2,1)} fusion(bf16[1024,512]{0,1:T(8,128)(2,1)S(1)} %bitcast.81, bf16[512,4096]{1,0:T(8,128)(2,1)} %all-gather.9.cloned.1.call-done), kind=kOutput, calls=%fused_computation.29 | convolution fusion | flops 4299161600 | bytes 13631488 | tf_op jit(solution)/shard_map/dot_general | solution.py:141
  273.0 0.6 copy-done.7
  273.5 0.1 copy.48
  273.6 0.1 sub.57
  273.7 5.1 convolution_convert_fusion.2
  278.8 6.7 %psum.29 = bf16[8,512]{1,0:T(8,128)(2,1)S(1)} all-reduce(bf16[8,512]{1,0:T(8,128)(2,1)S(1)} %convolution_convert_fusion.2), channel_id=1, replica_groups=mesh['psg'=8,'mp'=4] {'mp'}, use_global_device_ids=true, to_apply=%region_4.5 | all-reduce | flops 4096 | bytes 16384 | tf_op jit(solution)/shard_map/psum | solution.py:154
  285.5 0.1 multiply_reduce_fusion
  285.7 19.2 %psum.30 = f32[8]{0:T(128)S(1)} all-reduce(f32[8]{0:T(128)S(1)} %multiply_reduce_fusion), channel_id=1, replica_groups=mesh['psg'=8,'mp'=4] {'psg'}, use_global_device_ids=true, to_apply=%region_6.7 | all-reduce | flops 8 | bytes 64 | tf_op jit(solution)/shard_map/psum | solution.py:156
  304.9 0.4 fusion.52
  305.4 0.2 copy.62
  305.8 33.1 %psum.31 = f32[8,8,64]{2,0,1:T(8,128)S(1)} all-reduce(f32[8,8,64]{2,0,1:T(8,128)S(1)} %copy.49), channel_id=1, replica_groups=mesh['psg'=8,'mp'=4] {'psg'}, use_global_device_ids=true, to_apply=%region_7.8 | all-reduce | flops 4096 | bytes 32768 | tf_op jit(solution)/shard_map/psum | solution.py:158
  339.1 0.3 fusion.44
  339.4 31.5 %all_gather.29 = bf16[8,8,4096]{2,0,1:T(8,128)(2,1)S(1)} all-gather(bf16[8,8,512]{2,0,1:T(8,128)(2,1)S(1)} %fusion.44), channel_id=1, replica_groups=mesh['psg'=8,'mp'=4] {'psg'}, dimensions={2}, use_global_device_ids=true | all-gather | bytes 589824 | tf_op jit(solution)/shard_map/all_gather | solution.py:168
  370.9 53.5 %all-reduce.3.cloned.1.call-done = bf16[1024,4096]{1,0:T(8,128)(2,1)} async-done(((bf16[1024,4096]{1,0:T(8,128)(2,1)}), bf16[1024,4096]{1,0:T(8,128)(2,1)}) %all-reduce.3.cloned.1.call-update) | async-done | bytes 8388624 | tf_op jit(solution)/shard_map/psum | solution.py:146
  424.4 7.8 %fusion.4 = (f32[1024]{0:T(1024)S(1)}, bf16[1024,4096]{1,0:T(8,128)(2,1)S(1)}) fusion(bf16[1024,4096]{1,0:T(8,128)(2,1)} %all-reduce.3.cloned.1.call-done, bf16[1024,4096]{1,0:T(8,128)(2,1)} %param.18), kind=kLoop, calls=%fused_computation.14 | loop fusion | flops 29359104 | bytes 25169920 | tf_op jit(solution)/shard_map/reduce_sum | solution.py:74
  432.2 2.9 fusion.65
  435.2 0.3 copy-done.1
  435.4 6.4 %fusion.18 = f32[8,8,4096]{2,1,0:T(8,128)} fusion(bf16[1024,4096]{1,0:T(8,128)(2,1)S(1)} %get-tuple-element.200, f32[4096]{0:T(1024)S(1)} %copy-done.11, f32[1024]{0:T(1024)S(1)} %add_rsqrt_fusion, f32[8,8,1024]{2,1,0:T(8,128)S(1)} %get-tuple-element.209, f32[8,8]{1,0:T(8,128)S(1)} %get-tuple-element.208, pred[8,1024]{1,0:T(8,128)(4,1)S(1)} %broadcast_and_fusion), kind=kOutput, calls=%fused_computation.31 | convolution fusion | flops 3238133760 | bytes 9728256 | tf_op jit(solution)/shard_map/rht,td->rhd/dot_general | solution.py:178
  441.9 0.2 copy.52
  442.1 0.2 fusion.46
  442.3 31.6 %all-gather.1 = f32[64,8]{1,0:T(8,128)S(1)} all-gather(f32[8,8]{1,0:T(8,128)S(1)} %fusion.46), channel_id=3, replica_groups=mesh['psg'=8,'mp'=4] {'psg'}, dimensions={0}, use_global_device_ids=true | all-gather | bytes 2304 | tf_op jit(solution)/shard_map/all_gather | solution.py:29
  473.9 31.5 %all-gather = f32[64,8]{1,0:T(8,128)S(1)} all-gather(f32[8,8]{1,0:T(8,128)S(1)} %get-tuple-element.208), channel_id=2, replica_groups=mesh['psg'=8,'mp'=4] {'psg'}, dimensions={0}, use_global_device_ids=true | all-gather | bytes 2304 | tf_op jit(solution)/shard_map/all_gather | solution.py:29
  505.5 61.6 %all-gather.11.cloned.1.call-done = f32[64,8,4096]{2,1,0:T(8,128)} async-done(((f32[8,8,4096]{2,1,0:T(8,128)}), f32[64,8,4096]{2,1,0:T(8,128)}) %all-gather.11.cloned.1.call-update) | async-done | bytes 8388624 | tf_op jit(solution)/shard_map/all_gather | solution.py:29
  567.1 1.3 slice.65
  568.4 12.4 %while.19 = (s32[]{:T(128)}, f32[8,8]{1,0:T(8,128)S(1)}, f32[8,8]{1,0:T(8,128)S(1)}, f32[8,8,4096]{2,1,0:T(8,128)S(1)}, f32[8,8,8]{2,1,0:T(8,128)S(1)}, /*index=...) while((s32[]{:T(128)}, f32[8,8]{1,0:T(8,128)S(1)}, ...), condition=%wide.region_12.13_spmd, body=%wide.region_11.12_spmd.sunk | while | flops 786821 | bytes 3148439 | solution.py:35
  568.4 1.8 fusion.82
  570.3 1.7 fusion.82
  572.0 1.7 fusion.82
  573.8 1.7 fusion.82
  575.6 1.7 fusion.82
  577.3 1.7 fusion.82
  579.1 1.7 fusion.82
  580.8 0.1 dynamic-slice_divide_fusion
  580.9 0.5 convolution_bitcast_fusion
  581.4 0.6 collective-permute-start
  582.0 3.4 collective-permute-done
  585.4 3.9 collective-permute-done.1
  589.3 1.5 collective-permute-start.2
  590.8 3.3 collective-permute-done.2
  594.2 0.9 fusion.66
  595.2 3.1 constant_dynamic-slice_fusion
  598.2 14.8 %reduce-scatter.2.cloned.1.call-done = f32[8,128]{1,0:T(8,128)} async-done(((f32[8,512]{1,0:T(8,128)}), f32[8,128]{1,0:T(8,128)}) %reduce-scatter.2.cloned.1.call-update) | async-done | bytes 4112 | tf_op jit(solution)/shard_map/reduce_scatter | solution.py:194
  613.0 1.3 add_convert_fusion
  (69 shorter events, 1.3 us)
Async XLA Ops:
  7.2 297.7 %copy-start = (bf16[512,512]{1,0:T(8,128)(2,1)S(1)}, bf16[512,512]{1,0:T(8,128)(2,1)}, u32[]{:S(2)}) copy-start(bf16[512,512]{1,0:T(8,128)(2,1)} %param.30) | copy-start | bytes 1572868
  7.2 181.8 %all-gather.7.cloned.1.call-start = ((), (), s32[]{:S(2)}) async-start(), calls=%async_computation.1 | async-start | bytes 14155776 | tf_op jit(solution)/shard_map/all_gather | solution.py:119
  7.9 256.0 %all-gather.9.cloned.1.call-start = ((), (), s32[]{:S(2)}) async-start(), calls=%async_computation.2 | async-start | bytes 4718592 | tf_op jit(solution)/shard_map/all_gather | solution.py:143
  8.7 415.7 %all-reduce.3.cloned.1.call-start = ((), (), s32[]{:S(2)}) async-start(), calls=%async_computation.3 | async-start | bytes 16777216 | tf_op jit(solution)/shard_map/psum | solution.py:146
  12.6 12.1 %copy-start.9 = (s32[4]{0:T(128)S(1)}, s32[4]{0:T(128)}, u32[]{:S(2)}) copy-start(s32[4]{0:T(128)} %param.19) | copy-start | bytes 52
  20.5 168.5 %copy-start.10 = (f32[4096]{0:T(1024)S(1)}, f32[4096]{0:T(1024)}, u32[]{:S(2)}) copy-start(f32[4096]{0:T(1024)} %param.22) | copy-start | bytes 49156
  219.6 3.0 copy-start.3
  222.6 5.4 copy-start.2
  272.9 0.7 copy-start.7
  272.9 32.0 %copy-start.6 = (f32[512]{0:T(512)S(1)}, f32[512]{0:T(512)}, u32[]{:S(2)}) copy-start(f32[512]{0:T(512)} %param.29) | copy-start | bytes 6148
  272.9 32.4 %copy-start.4 = (bf16[2,512,512]{2,1,0:T(8,128)(2,1)S(1)}, bf16[2,512,512]{2,1,0:T(8,128)(2,1)}, u32[]{:S(2)}) copy-start(bf16[2,512,512]{2,1,0:T(8,128)(2,1)} %param.31) | copy-start | bytes 3145732
  272.9 294.2 %all-gather.11.cloned.1.call-start = ((), (), s32[]{:S(2)}) async-start(), calls=%async_computation.5 | async-start | bytes 9437184 | tf_op jit(solution)/shard_map/all_gather | solution.py:29
  273.7 31.9 %copy-start.8 = (f32[4]{0:T(128)S(1)}, f32[4]{0:T(128)}, u32[]{:S(2)}) copy-start(f32[4]{0:T(128)} %param.21) | copy-start | bytes 52
  273.7 65.2 %copy-start.12 = (s32[4]{0:T(128)S(1)}, s32[4]{0:T(128)}, u32[]{:S(2)}) copy-start(s32[4]{0:T(128)} %param.20) | copy-start | bytes 52
  370.9 61.3 %copy-start.11 = (f32[4096]{0:T(1024)S(1)}, f32[4096]{0:T(1024)}, u32[]{:S(2)}) copy-start(f32[4096]{0:T(1024)} %param.26) | copy-start | bytes 49156
  432.2 3.2 copy-start.1
  441.9 171.2 %reduce-scatter.2.cloned.1.call-start = ((), (), s32[]{:S(2)}) async-start(), calls=%async_computation.4 | async-start | bytes 20480 | tf_op jit(solution)/shard_map/reduce_scatter | solution.py:194
  568.4 25.8 %copy-start.5 = (bf16[512,512]{1,0:T(8,128)(2,1)S(1)}, bf16[512,512]{1,0:T(8,128)(2,1)}, u32[]{:S(2)}) copy-start(bf16[512,512]{1,0:T(8,128)(2,1)} %param.32) | copy-start | bytes 1572868
  581.4 3.9 collective-permute-start
  585.4 3.9 collective-permute-start.1
  589.3 4.8 collective-permute-start.2
Sparse Core Ops, SparseCore 0:
  10.2 178.8 all-gather.6
  191.1 72.8 all-gather.8
  273.0 151.3 all-reduce.2
  442.0 125.0 all-gather.10
  595.3 17.7 reduce-scatter.1
